TPU v7x, 128 devices: a whole 4x4x4 slice. The times are simulated.
128 devices in a mesh: row: 8 (over y_hi, z), col: 16 (over x, y_lo, core).
Axes of the slice: x: 4, y: 4 (y_hi: 2, y_lo: 2; y = y_hi * 2 + y_lo), z: 4, core: 2. Of those that a mesh axis runs over, the one named last changes fastest.
Arguments:
- a_panels: float32 [8192, 4096], P('row', 'col'), may hold values from -6 to 6
- b_panels: float32 [4096, 32768], P('row', 'col'), may hold values from -0.1875 to 0.1875
- a_occupancy: int32 [64, 32], P('row', 'col'), may hold values 0 or 1
- b_occupancy: int32 [32, 256], P('row', 'col'), may hold values 0 or 1
- owner_device: int32 [8, 16, 128, 1], P('row', 'col'), may hold values from 0 to 127; in each aligned block of 128 rows (0 to 127, 128 to 255, ..., all dimensions but the last counted through in order) at most 2 rows name the same one
- owner_block: int32 [8, 16, 128], P('row', 'col'), may hold values from 0 to 127
- c_previous: float32 [8, 16, 128, 128, 128], P('row', 'col'), may hold values from -6 to 6
Outputs:
- c_owned: float32 [8, 16, 128, 128, 128], P('row', 'col')
Inputs may be any that keep to these rules, and one draw needn't show every extreme that they name: `owner_device`: among the 128 product blocks of one device, at most 2 name the same owner; some owner is named exactly 2 times by one device.
All inputs are finite; a program needn't handle non-finite values. No bound on the sum of `a_occupancy` or of `b_occupancy` on one device may be relied on, other than what follows from the above.
Results may differ from a plain program's by a relative error of at most 0.0003.
Values sent between devices are 32-bit elements; how exact they have to be, the bound alone decides.
A program may use at most 192 MiB of HBM per device.

v0:
```python
import jax
import jax.numpy as jnp
from jax import lax
from jax.sharding import PartitionSpec as P

BLK = 128
TICKS = 4


def shifted(value, axis, steps):
    count = lax.axis_size(axis)
    pairs = [(source, (source + steps) % count) for source in range(count)]
    return lax.ppermute(value, axis, pairs)


def widen(occupancy, panel):
    return panel * jnp.repeat(jnp.repeat(occupancy.astype(jnp.float32), BLK, axis=0), BLK, axis=1)


def multiply(left, right):
    return jnp.dot(left, right, preferred_element_type=jnp.float32, precision=lax.Precision.HIGHEST)


def pick_image(held, tick, n_row, n_col):
    images = n_col // n_row
    inner = held.shape[0] // images
    slot = (lax.axis_index("row") + lax.axis_index("col") + tick) % n_col // n_row
    return lax.dynamic_slice_in_dim(held, slot * inner, inner, 0)


def per_device(a_panels, b_panels, a_occupancy, b_occupancy, owner_device, owner_block, c_previous):
    n_row = lax.axis_size("row")
    n_col = lax.axis_size("col")
    left = widen(a_occupancy, a_panels)
    right = widen(b_occupancy, b_panels)
    acc = jnp.zeros((left.shape[0], right.shape[1]), jnp.float32)
    for tick in range(TICKS):
        acc = acc + multiply(left, pick_image(right, tick, n_row, n_col))
        if tick + 1 < TICKS:
            left = shifted(left, "col", -1)
            right = shifted(right, "row", -1)
    rows_blocks = left.shape[0] // BLK
    cols_blocks = right.shape[1] // BLK
    count_blocks = rows_blocks * cols_blocks
    pieces = (
        acc.reshape(rows_blocks, BLK, cols_blocks, BLK)
        .transpose(0, 2, 1, 3)
        .reshape(count_blocks, BLK, BLK)
    )
    devices_all = n_row * n_col
    capacity = max(2, (2 * count_blocks + devices_all - 1) // devices_all)
    owners = owner_device.reshape(count_blocks)
    targets = owner_block.reshape(count_blocks)
    onehot = (owners[:, None] == jnp.arange(devices_all, dtype=jnp.int32)[None, :]).astype(
        jnp.int32
    )
    earlier = jnp.cumsum(onehot, axis=0) - onehot
    ranks = jnp.sum(earlier * onehot, axis=1)
    places = owners * capacity + ranks
    send_blocks = jnp.zeros((devices_all * capacity, BLK, BLK), jnp.float32).at[places].set(pieces)
    send_targets = (
        jnp.full((devices_all * capacity,), -1.0, jnp.float32)
        .at[places]
        .set(targets.astype(jnp.float32))
    )
    got_blocks, got_targets = (
        lax.all_to_all(
            send_blocks.reshape(devices_all, capacity, BLK, BLK),
            ("row", "col"),
            split_axis=0,
            concat_axis=0,
            tiled=True,
        ),
        lax.all_to_all(
            send_targets.reshape(devices_all, capacity),
            ("row", "col"),
            split_axis=0,
            concat_axis=0,
            tiled=True,
        ),
    )
    flat_blocks = got_blocks.reshape(devices_all * capacity, BLK * BLK)
    flat_targets = got_targets.reshape(devices_all * capacity)
    owned = c_previous.shape[2]
    select = (jnp.arange(owned, dtype=jnp.float32)[:, None] == flat_targets[None, :]).astype(
        jnp.float32
    )
    added = jnp.dot(
        select, flat_blocks, preferred_element_type=jnp.float32, precision=lax.Precision.HIGHEST
    )
    result = c_previous.reshape(owned, BLK * BLK) + added
    return result.reshape(c_previous.shape)


def solution(mesh):
    in_specs = (
        P("row", "col"),
        P("row", "col"),
        P("row", "col"),
        P("row", "col"),
        P("row", "col", None, None),
        P("row", "col", None),
        P("row", "col", None, None, None),
    )
    out_specs = P("row", "col", None, None, None)
    return jax.shard_map(
        per_device, mesh=mesh, in_specs=in_specs, out_specs=out_specs, check_vma=False
    )
```

profile of v0, /device:TPU:18, one launch (start us, length us, event | category | flops | bytes accessed | tf_op | source)
XLA Modules:
  0.0 702.6 jit_solution(10438058538702257088)
XLA Ops:
  0.0 0.7 convert_element_type.20
  0.7 0.0 copy-start.4
  0.7 1.1 broadcast_in_dim.27
  1.9 0.0 copy-start.1
  1.9 0.0 copy-start.3
  1.9 0.0 copy-start.5
  1.9 4.5 bitcast_multiply_fusion
  6.4 0.0 copy-start
  6.5 2.0 copy-done
  8.5 3.8 collective-permute-start.1
  12.3 89.8 %collective-permute-done.1 = f32[512,2048]{1,0:T(8,128)S(1)} collective-permute-done((f32[512,2048]{1,0:T(8,128)S(1)}, f32[512,2048]{1,0:T(8,128)S(1)}, u32[]{:S(2)}, u32[]{:S(2)}) %collective-permute-start.1) | collective-permute-done | bytes 4194336 | tf_op jit(solution)/shard_map/ppermute | solution.py:13
  102.1 0.0 copy-start.2
  102.1 1.9 copy-done.2
  104.0 6.1 collective-permute-start.3
  110.1 89.0 %collective-permute-done.3 = f32[512,2048]{1,0:T(8,128)} collective-permute-done((f32[512,2048]{1,0:T(8,128)S(1)}, f32[512,2048]{1,0:T(8,128)}, u32[]{:S(2)}, u32[]{:S(2)}) %collective-permute-start.3) | collective-permute-done | bytes 4194336 | tf_op jit(solution)/shard_map/ppermute | solution.py:13
  199.1 6.2 collective-permute-start.5
  205.3 0.0 copy-done.4
  205.3 0.1 copy.12
  205.4 1.2 broadcast_in_dim.25
  206.7 0.0 copy-done.1
  206.7 0.1 bitcast_multiply_fusion.1
  206.8 0.1 collective-permute-start
  206.9 12.4 %collective-permute-done = f32[1024,256]{1,0:T(8,128)S(1)} collective-permute-done((f32[1024,256]{1,0:T(8,128)S(1)}, f32[1024,256]{1,0:T(8,128)S(1)}, u32[]{:S(2)}, u32[]{:S(2)}) %collective-permute-start) | collective-permute-done | bytes 1048608 | tf_op jit(solution)/shard_map/ppermute | solution.py:13
  219.3 2.9 collective-permute-start.2
  222.1 0.0 copy-done.3
  222.1 0.1 fusion.13
  222.2 0.2 reduce_window_sum.11
  222.4 0.2 select_reduce_fusion
  222.6 0.0 copy-done.5
  222.6 1.0 scatter_custom_fusion
  223.6 0.8 all_to_all.9
  224.4 92.7 %all-to-all-start = ((f32[128,1,2]{2,1,0:T(1,128)}), f32[128,1,2]{2,1,0:T(1,128)}, u32[]{:S(2)}, u32[]{:S(2)}) async-start(f32[128,1,2]{2,1,0:T(1,128)} %bitcast.5), calls=%async_computation | async-start | bytes 131072 | tf_op jit(solution)/shard_map/all_to_all | solution.py:74
  317.1 0.0 collective-permute-done.2
  317.1 1.3 collective-permute-start.4
  318.4 10.2 %fusion.10 = f32[1024,2048]{1,0:T(8,128)} fusion(f32[1024,256]{1,0:T(8,128)S(1)} %bitcast_multiply_fusion.1, f32[512,2048]{1,0:T(8,128)} %copy-done, s32[]{:T(128)S(6)} %select_n.58), kind=kOutput, calls=%fused_computation.13 | convolution fusion | flops 6442450944 | bytes 11534340 | tf_op jit(solution)/shard_map/dot_general | solution.py:21
  328.5 0.0 slice-start
  328.5 9.2 %fusion.8 = f32[1024,2048]{1,0:T(8,128)S(1)} fusion(f32[1024,256]{1,0:T(8,128)S(1)} %collective-permute-done, f32[512,2048]{1,0:T(8,128)} %copy-done.2, s32[]{:T(128)S(6)} %select_n.61), kind=kOutput, calls=%fused_computation.11 | convolution fusion | flops 6442450944 | bytes 11534340 | tf_op jit(solution)/shard_map/dot_general | solution.py:21
  337.8 0.0 slice-start.1
  337.8 11.4 %fusion.6 = f32[1024,2048]{1,0:T(8,128)} fusion(f32[1024,256]{1,0:T(8,128)} %collective-permute-done.2, f32[512,2048]{1,0:T(8,128)} %collective-permute-done.3, s32[]{:T(128)S(6)} %select_n.64), kind=kOutput, calls=%fused_computation.9 | convolution fusion | flops 6442450944 | bytes 11534340 | tf_op jit(solution)/shard_map/dot_general | solution.py:21
  349.2 0.0 collective-permute-done.4
  349.2 0.0 collective-permute-done.5
  349.2 0.0 slice-done
  349.2 0.0 slice-done.1
  349.2 13.8 %add_bitcast_fusion = f32[128,8,16,128]{3,1,2,0:T(8,128)} fusion(f32[1024,2048]{1,0:T(8,128)} %fusion.6, f32[1024,2048]{1,0:T(8,128)S(1)} %bitcast.51, f32[1024,2048]{1,0:T(8,128)S(1)} %fusion.8, f32[1024,256]{1,0:T(8,128)} %collective-permute-done.4, f32[512,2048]{1,0:T(8,128)} %collective-permute-done.5, s32[]{:T(128)S(6)} %select_n.67), kind=kOutput, calls=%fused_computation.5 | convolution fusion | flops 6448742400 | bytes 36700164 | tf_op jit(solution)/shard_map/dot_general | solution.py:21
  363.0 5.4 copy.17
  368.4 5.9 copy.13
  374.3 7.9 %broadcast_in_dim.23 = f32[256,128,128]{2,1,0:T(8,128)} broadcast(f32[]{:T(128)} %constant.79.clone.1), dimensions={} | broadcast | bytes 16777220 | tf_op jit(solution)/shard_map/broadcast_in_dim | solution.py:60
  382.1 23.4 %scatter_fusion = f32[256,128,128]{2,1,0:T(8,128)} fusion(f32[256,128,128]{2,1,0:T(8,128)} %broadcast_in_dim.23, s32[128]{0:T(128)S(1)} %fusion.18, f32[128,128,128]{2,1,0:T(8,128)} %bitcast.52), kind=kCustom, calls=%fused_computation.1 | custom fusion | bytes 25166336 | tf_op jit(solution)/shard_map/scatter | solution.py:60
  405.6 0.0 all-to-all-done
  405.6 12.4 %all-to-all-start.1 = ((f32[128,2,128,128]{3,2,1,0:T(8,128)}), f32[128,2,128,128]{3,2,1,0:T(8,128)}, u32[]{:S(2)}, u32[]{:S(2)}) async-start(f32[128,2,128,128]{3,2,1,0:T(8,128)} %bitcast.49), calls=%async_computation.1 | async-start | bytes 33554432 | tf_op jit(solution)/shard_map/all_to_all | solution.py:67
  417.9 0.5 broadcast.49
  418.4 1.6 reduce.3
  420.1 0.1 eq.40
  420.2 246.4 %all-to-all-done.1 = f32[128,2,128,128]{3,2,1,0:T(8,128)} async-done(((f32[128,2,128,128]{3,2,1,0:T(8,128)}), f32[128,2,128,128]{3,2,1,0:T(8,128)}, u32[]{:S(2)}, u32[]{:S(2)}) %all-to-all-start.1) | async-done | bytes 16777248 | tf_op jit(solution)/shard_map/all_to_all | solution.py:67
  666.6 27.5 %fusion.2 = f32[16,8,128,128]{3,1,2,0:T(8,128)} fusion(f32[32,8,128,128]{3,2,1,0:T(8,128)} %bitcast.23, f32[16,8,128,128]{3,2,1,0:T(8,128)} %bitcast.55, f32[256]{0:T(256)S(1)} %eq.40), kind=kOutput, calls=%fused_computation.7 | convolution fusion | flops 6444580864 | bytes 33555456 | tf_op jit(solution)/shard_map/dot_general | solution.py:88
  694.1 8.2 %copy.19 = f32[16,8,128,128]{3,2,1,0:T(8,128)} copy(f32[16,8,128,128]{3,1,2,0:T(8,128)} %fusion.2) | data formatting | bytes 16777216
  (6 shorter events, 0.1 us)
Async XLA Ops:
  0.7 204.6 %copy-start.4 = (s32[8,2]{0,1:T(2,128)S(1)}, s32[8,2]{0,1:T(2,128)}, u32[]{:S(2)}) copy-start(s32[8,2]{0,1:T(2,128)} %param.9) | copy-start | bytes 196
  1.9 204.8 %copy-start.1 = (f32[1024,256]{1,0:T(8,128)S(1)}, f32[1024,256]{1,0:T(8,128)}, u32[]{:S(2)}) copy-start(f32[1024,256]{1,0:T(8,128)} %param.7) | copy-start | bytes 3145732
  1.9 220.3 %copy-start.3 = (s32[1,1,128,1]{2,3,1,0:T(1,128)S(1)}, s32[1,1,128,1]{2,3,1,0:T(1,128)}, u32[]{:S(2)}) copy-start(s32[1,1,128,1]{2,3,1,0:T(1,128)} %param.11) | copy-start | bytes 1540
  1.9 220.7 %copy-start.5 = (s32[1,1,128]{2,1,0:T(1,128)S(1)}, s32[1,1,128]{2,1,0:T(1,128)}, u32[]{:S(2)}) copy-start(s32[1,1,128]{2,1,0:T(1,128)} %param.12) | copy-start | bytes 1540
  6.4 2.0 copy-start
  8.5 93.6 %collective-permute-start.1 = (f32[512,2048]{1,0:T(8,128)S(1)}, f32[512,2048]{1,0:T(8,128)S(1)}, u32[]{:S(2)}, u32[]{:S(2)}) collective-permute-start(f32[512,2048]{1,0:T(8,128)S(1)} %bitcast_multiply_fusion), channel_id=1, source_target_pairs={{0,112},{16,0},{32,16},{48,32},{64,48},{80,64},{96,80},{112,96},{1... | collective-permute-start | bytes 12582920 | tf_op jit(solution)/shard_map/ppermute | solution.py:13
  102.1 1.9 copy-start.2
  104.0 95.1 %collective-permute-start.3 = (f32[512,2048]{1,0:T(8,128)S(1)}, f32[512,2048]{1,0:T(8,128)}, u32[]{:S(2)}, u32[]{:S(2)}) collective-permute-start(f32[512,2048]{1,0:T(8,128)S(1)} %collective-permute-done.1), channel_id=1, source_target_pairs={{0,112},{16,0},{32,16},{48,32},{64,48},{80,64},{96,80},{112,96},{1... | collective-permute-start | bytes 12582920 | tf_op jit(solution)/shard_map/ppermute | solution.py:13
  199.1 150.1 %collective-permute-start.5 = (f32[512,2048]{1,0:T(8,128)}, f32[512,2048]{1,0:T(8,128)}, u32[]{:S(2)}, u32[]{:S(2)}) collective-permute-start(f32[512,2048]{1,0:T(8,128)} %collective-permute-done.3), channel_id=1, source_target_pairs={{0,112},{16,0},{32,16},{48,32},{64,48},{80,64},{96,80},{112,96},{1... | collective-permute-start | bytes 12582920 | tf_op jit(solution)/shard_map/ppermute | solution.py:13
  206.8 12.4 %collective-permute-start = (f32[1024,256]{1,0:T(8,128)S(1)}, f32[1024,256]{1,0:T(8,128)S(1)}, u32[]{:S(2)}, u32[]{:S(2)}) collective-permute-start(f32[1024,256]{1,0:T(8,128)S(1)} %bitcast_multiply_fusion.1), channel_id=1, source_target_pairs={{0,15},{1,0},{2,1},{3,2},{4,3},{5,4},{6,5},{7,6},{8,7},{9,8},{10,9... | collective-permute-start | bytes 3145736 | tf_op jit(solution)/shard_map/ppermute | solution.py:13
  219.3 97.8 %collective-permute-start.2 = (f32[1024,256]{1,0:T(8,128)S(1)}, f32[1024,256]{1,0:T(8,128)}, u32[]{:S(2)}, u32[]{:S(2)}) collective-permute-start(f32[1024,256]{1,0:T(8,128)S(1)} %collective-permute-done), channel_id=1, source_target_pairs={{0,15},{1,0},{2,1},{3,2},{4,3},{5,4},{6,5},{7,6},{8,7},{9,8},{10,9... | collective-permute-start | bytes 3145736 | tf_op jit(solution)/shard_map/ppermute | solution.py:13
  224.4 181.2 %all-to-all-start = ((f32[128,1,2]{2,1,0:T(1,128)}), f32[128,1,2]{2,1,0:T(1,128)}, u32[]{:S(2)}, u32[]{:S(2)}) async-start(f32[128,1,2]{2,1,0:T(1,128)} %bitcast.5), calls=%async_computation | async-start | bytes 131072 | tf_op jit(solution)/shard_map/all_to_all | solution.py:74
  317.1 32.1 %collective-permute-start.4 = (f32[1024,256]{1,0:T(8,128)}, f32[1024,256]{1,0:T(8,128)}, u32[]{:S(2)}, u32[]{:S(2)}) collective-permute-start(f32[1024,256]{1,0:T(8,128)} %collective-permute-done.2), channel_id=1, source_target_pairs={{0,15},{1,0},{2,1},{3,2},{4,3},{5,4},{6,5},{7,6},{8,7},{9,8},{10,9... | collective-permute-start | bytes 3145736 | tf_op jit(solution)/shard_map/ppermute | solution.py:13
  328.5 20.6 %slice-start = ((s8[8388608]{0:T(1024)(128)(4,1)}), s8[4194304]{0:T(1024)(128)(4,1)S(1)}, s32[]{:S(2)}) async-start(s8[8388608]{0:T(1024)(128)(4,1)} %bitcast.50), calls=%async_computation.2 | async-start | bytes 8388608
  337.8 11.4 %slice-start.1 = ((s8[8388608]{0:T(1024)(128)(4,1)}), s8[4194304]{0:T(1024)(128)(4,1)S(1)}, s32[]{:S(2)}) async-start(s8[8388608]{0:T(1024)(128)(4,1)} %bitcast.50), calls=%async_computation.3 | async-start | bytes 8388608
  405.6 261.0 %all-to-all-start.1 = ((f32[128,2,128,128]{3,2,1,0:T(8,128)}), f32[128,2,128,128]{3,2,1,0:T(8,128)}, u32[]{:S(2)}, u32[]{:S(2)}) async-start(f32[128,2,128,128]{3,2,1,0:T(8,128)} %bitcast.49), calls=%async_computation.1 | async-start | bytes 33554432 | tf_op jit(solution)/shard_map/all_to_all | solution.py:67
where the time goes:
time: 709 us; the launch traced here: 703 us
  waiting for transfers between devices  438 us (62%)
  starting transfers between devices  125 us (18%)
  matrix products  72 us (10%)
  local copies, waits for them, and re-layouts  59.7 us (8%)
  other arithmetic  7.45 us (1%)
    all_to_all x1, waiting for transfers between devices, per_device(): lax.all_to_all(send_blocks.reshape(devices_all, capacity, BLK, BLK), ('ro...  246 us
    ppermute x6, waiting for transfers between devices, shifted(): return lax.ppermute(value, axis, pairs)  191 us
    all_to_all x1, starting transfers between devices, per_device(): lax.all_to_all(send_targets.reshape(devices_all, capacity), ('row', 'col'...  92.7 us
    dot_general x4, matrix products, multiply(): jnp.dot(left, right, preferred_element_type=jnp.float32, precision=lax.Pr...  44.5 us
    dot_general x1, matrix products, per_device(): jnp.dot(select, flat_blocks, preferred_element_type=jnp.float32, precisio...  27.5 us
    scatter x1, local copies, waits for them, and re-layouts, per_device(): jnp.zeros((devices_all * capacity, BLK, BLK), jnp.float32).at[places]  23.4 us
    ppermute x6, starting transfers between devices, shifted(): return lax.ppermute(value, axis, pairs)  20.3 us
    unnamed x18, local copies, waits for them, and re-layouts  17.6 us
  transfers between devices with their start and end apart: 8, of which 4 were waited for; matrix products, arithmetic and copies ran while one was open for 13% of the time, Pallas kernels for 0%

commit v1 on v0

v1 whole, which is shorter than its diff:
```python
import jax
import jax.numpy as jnp
from jax import lax
from jax.experimental import pallas as pl
from jax.experimental.pallas import tpu as pltpu
from jax.sharding import PartitionSpec as P

BLK = 128
TICKS = 4
N_ROW = 8
N_COL = 16
DEVICES = N_ROW * N_COL
NBLK = 128
CHUNKS = 4
MESH = pl.DeviceIdType.MESH
VMEM_LIMIT = 64 * 1024 * 1024 - 65536


def product_kernel(
    a_ref, b_ref, a_occ, b_occ, inv, s_out,
    a_own, b_own, b_cross, b_far, a_got, b_got, a_cat, b_cat, prod, staged,
    a_send, a_recv, b_send, b_recv, x_send, x_recv, out_sem,
):
    row = lax.axis_index("row")
    col = lax.axis_index("col")
    half = row // 4
    z = row % 4
    far = (row + 4) % N_ROW
    inner = b_ref.shape[0] // 2
    part = inner // CHUNKS

    barrier = pltpu.get_barrier_semaphore()
    peers = [(half * 4 + (z + d) % 4, col) for d in (1, 2, 3)]
    peers.append((far, col))
    peers += [(row, (col + d) % N_COL) for d in (1, 2, 3, 13, 14, 15)]
    for peer in peers:
        pl.semaphore_signal(barrier, inc=1, device_id=peer, device_id_type=MESH)

    slot_own = ((row + col) % N_COL) // N_ROW
    slot_cross = ((row + 8 * (1 - half) + col) % N_COL) // N_ROW

    def mask_right(slot, into):
        def one(n, carry):
            k = n // 16
            q = n % 16
            there = b_occ[slot * 2 + k, q].astype(jnp.float32)
            at = pl.multiple_of(q * BLK, BLK)
            into[pl.ds(k * BLK, BLK), pl.ds(at, BLK)] = (
                b_ref[pl.ds(slot * inner + k * BLK, BLK), pl.ds(at, BLK)] * there
            )
            return carry

        lax.fori_loop(0, 32, one, 0)

    mask_right(slot_cross, b_cross)
    pl.semaphore_wait(barrier, len(peers))

    def cross_copy(c):
        rows = pl.ds(c * part, part)
        return pltpu.make_async_remote_copy(
            b_cross.at[rows], b_far.at[rows], x_send.at[c], x_recv.at[c],
            device_id=(far, col), device_id_type=MESH,
        )

    def ring_copy(source, t, rows):
        return pltpu.make_async_remote_copy(
            source.at[rows], b_got.at[t - 1, rows], b_send.at[t - 1], b_recv.at[t - 1],
            device_id=(half * 4 + (z + 4 - t) % 4, col), device_id_type=MESH,
        )

    def left_copy(t):
        return pltpu.make_async_remote_copy(
            a_own, a_got.at[t - 1], a_send.at[t - 1], a_recv.at[t - 1],
            device_id=(row, (col + N_COL - t) % N_COL), device_id_type=MESH,
        )

    @pl.when(z < 3)
    def _():
        for c in range(CHUNKS):
            cross_copy(c).start()

    mask_right(slot_own, b_own)
    for t in (1, 2, 3):
        @pl.when(z >= t)
        def _(t=t):
            ring_copy(b_own, t, pl.ds(0, inner)).start()

    def mask_left(n, carry):
        p = n // 2
        for k in range(2):
            there = a_occ[p, k].astype(jnp.float32)
            at = pl.ds(p * BLK, BLK)
            a_own[at, k * BLK:(k + 1) * BLK] = a_ref[at, k * BLK:(k + 1) * BLK] * there
        return carry

    lax.fori_loop(0, 16, mask_left, 0)
    for t in (1, 2, 3):
        left_copy(t).start()

    def split_left(read):
        def one(m, carry):
            at = pl.ds(m * BLK, BLK)
            value = read(at)
            high = value.astype(jnp.bfloat16)
            low = (value - high.astype(jnp.float32)).astype(jnp.bfloat16)
            a_cat[at, 0:256] = high
            a_cat[at, 256:512] = high
            a_cat[at, 512:768] = low
            return carry

        lax.fori_loop(0, 8, one, 0)

    def split_right(read):
        def one(n, carry):
            at = pl.ds(pl.multiple_of(n * BLK, BLK), BLK)
            value = read(at)
            high = value.astype(jnp.bfloat16)
            low = (value - high.astype(jnp.float32)).astype(jnp.bfloat16)
            b_cat[0:256, at] = high
            b_cat[256:512, at] = low
            b_cat[512:768, at] = high
            return carry

        lax.fori_loop(0, 16, one, 0)

    def multiply(first):
        def one(step, carry):
            n = step // 4
            m = step % 4
            columns = pl.ds(pl.multiple_of(n * 256, 256), 256)
            tile = jnp.dot(
                a_cat[pl.ds(pl.multiple_of(m * 256, 256), 256), :], b_cat[:, columns],
                preferred_element_type=jnp.float32,
            )
            for h in range(2):
                at = pl.ds((2 * n + h) * 8 + 2 * m, 2)
                block = tile[:, h * BLK:(h + 1) * BLK].reshape(2, BLK, BLK)
                prod[at] = block if first else prod[at] + block
            return carry

        lax.fori_loop(0, 32, one, 0)

    split_left(lambda at: a_own[at, :])
    split_right(lambda at: b_own[:, at])
    multiply(True)

    @pl.when(z < 3)
    def _():
        for c in range(CHUNKS):
            cross_copy(c).wait_recv()
            for t in (1, 2, 3):
                @pl.when(z < t)
                def _(t=t):
                    ring_copy(b_far, t, pl.ds(c * part, part)).start()
        for c in range(CHUNKS):
            cross_copy(c).wait_send()

    for t in (1, 2, 3):
        left_copy(t).wait_recv()
        split_left(lambda at: a_got[t - 1, at, :])
        ring_copy(b_own, t, pl.ds(0, inner)).wait_recv()
        split_right(lambda at: b_got[t - 1, :, at])
        multiply(False)

    def place(group, carry):
        for k in range(16):
            n = group * 16 + k
            staged[n] = prod[inv[n]]
        at = pl.ds(group * 16, 16)
        pltpu.make_async_copy(staged.at[at], s_out.at[at], out_sem).start()
        return carry

    lax.fori_loop(0, 16, place, 0)
    for t in (1, 2, 3):
        left_copy(t).wait_send()
        ring_copy(b_own, t, pl.ds(0, inner)).wait_send()
    pltpu.make_async_copy(staged, s_out, out_sem).wait()


def add_kernel(targets, c_ref, got_ref, out_ref):
    step = pl.program_id(0)
    count = got_ref.shape[0]

    @pl.when(step == 0)
    def _():
        out_ref[...] = c_ref[...]

    def one(k, carry):
        target = targets[step * count + k]

        @pl.when(target >= 0)
        def _():
            out_ref[target] = out_ref[target] + got_ref[k]

        return carry

    lax.fori_loop(0, count, one, 0)


def per_device(a_panels, b_panels, a_occupancy, b_occupancy, owner_device, owner_block, c_previous):
    owners = owner_device.reshape(NBLK)
    targets = owner_block.reshape(NBLK)
    number = jnp.arange(NBLK, dtype=jnp.int32)
    named = owners[:, None] == jnp.arange(DEVICES, dtype=jnp.int32)[None, :]
    packed = number * DEVICES + targets
    first = jnp.min(jnp.where(named, packed[:, None], NBLK * DEVICES), axis=0)
    last = jnp.max(jnp.where(named, packed[:, None], -1), axis=0)
    has_first = last >= 0
    has_second = last > first
    pair = jnp.stack([jnp.where(has_first, first, 0), jnp.where(has_second, last, 0)], axis=1)
    there = jnp.stack([has_first, has_second], axis=1)
    block = pair // DEVICES
    inv = ((block % 16) * 8 + block // 16).reshape(2 * DEVICES)
    send_targets = jnp.where(there, pair % DEVICES, -1)
    got_targets = lax.all_to_all(
        send_targets, ("row", "col"), split_axis=0, concat_axis=0, tiled=True
    )

    vmem = lambda shape, dtype=jnp.float32: pltpu.VMEM(shape, dtype)
    send = pl.pallas_call(
        product_kernel,
        out_shape=jax.ShapeDtypeStruct((2 * DEVICES, BLK, BLK), jnp.float32),
        in_specs=[
            pl.BlockSpec(memory_space=pltpu.VMEM),
            pl.BlockSpec(memory_space=pltpu.VMEM),
            pl.BlockSpec(memory_space=pltpu.SMEM),
            pl.BlockSpec(memory_space=pltpu.SMEM),
            pl.BlockSpec(memory_space=pltpu.SMEM),
        ],
        out_specs=pl.BlockSpec(memory_space=pl.ANY),
        scratch_shapes=[
            vmem((1024, 256)), vmem((256, 2048)), vmem((256, 2048)), vmem((256, 2048)),
            vmem((3, 1024, 256)), vmem((3, 256, 2048)),
            vmem((1024, 768), jnp.bfloat16), vmem((768, 2048), jnp.bfloat16),
            vmem((NBLK, BLK, BLK)), vmem((2 * DEVICES, BLK, BLK)),
            pltpu.SemaphoreType.DMA((3,)), pltpu.SemaphoreType.DMA((3,)),
            pltpu.SemaphoreType.DMA((3,)), pltpu.SemaphoreType.DMA((3,)),
            pltpu.SemaphoreType.DMA((CHUNKS,)), pltpu.SemaphoreType.DMA((CHUNKS,)),
            pltpu.SemaphoreType.DMA,
        ],
        compiler_params=pltpu.CompilerParams(
            collective_id=0, has_side_effects=True, vmem_limit_bytes=VMEM_LIMIT
        ),
        name="products",
    )(a_panels, b_panels, a_occupancy, b_occupancy, inv)

    got = lax.all_to_all(
        send.reshape(DEVICES, 2, BLK, BLK), ("row", "col"), split_axis=0, concat_axis=0, tiled=True
    ).reshape(2 * DEVICES, BLK, BLK)

    owned = pl.pallas_call(
        add_kernel,
        out_shape=jax.ShapeDtypeStruct((NBLK, BLK, BLK), jnp.float32),
        grid_spec=pltpu.PrefetchScalarGridSpec(
            num_scalar_prefetch=1,
            grid=(16,),
            in_specs=[
                pl.BlockSpec((NBLK, BLK, BLK), lambda i, t: (0, 0, 0)),
                pl.BlockSpec((16, BLK, BLK), lambda i, t: (i, 0, 0)),
            ],
            out_specs=pl.BlockSpec((NBLK, BLK, BLK), lambda i, t: (0, 0, 0)),
        ),
        compiler_params=pltpu.CompilerParams(vmem_limit_bytes=VMEM_LIMIT),
        name="add_blocks",
    )(got_targets.reshape(2 * DEVICES), c_previous.reshape(NBLK, BLK, BLK), got)
    return owned.reshape(c_previous.shape)


def solution(mesh):
    in_specs = (
        P("row", "col"),
        P("row", "col"),
        P("row", "col"),
        P("row", "col"),
        P("row", "col", None, None),
        P("row", "col", None),
        P("row", "col", None, None, None),
    )
    out_specs = P("row", "col", None, None, None)
    return jax.shard_map(
        per_device, mesh=mesh, in_specs=in_specs, out_specs=out_specs, check_vma=False
    )
```

time: 709 us -> 487 us (0.69)
  waiting for transfers between devices: 438 us -> 243 us
  Pallas kernels: 0 us -> 174 us
  matrix products: 72 us -> 0 us
  starting transfers between devices: 125 us -> 57.2 us
  local copies, waits for them, and re-layouts: 59.7 us -> 3.56 us
    ppermute x6 -> x0, waiting for transfers between devices: 191 us -> none  [shifted(): return lax.ppermute(value, axis, pairs)]
    pallas_call x0 -> x2, Pallas kernels: none -> 174 us  [the longest x1 153 us: per_device(): pl.pallas_call(product_kernel, out_shape=jax.ShapeDtypeStruct((2 * DEVICE...]
    dot_general x5 -> x0, matrix products: 72 us -> none  [the longest x4 44.5 us: multiply(): jnp.dot(left, right, preferred_element_type=jnp.float32, precision=lax.Pr...]
    all_to_all x2, starting transfers between devices: 105 us -> 57.2 us  [the longest x1 46.5 us: per_device(): lax.all_to_all(send.reshape(DEVICES, 2, BLK, BLK), ('row', 'col'), split_...]
    scatter x2 -> x0, local copies, waits for them, and re-layouts: 24.4 us -> none  [the longest x1 23.4 us: per_device(): jnp.zeros((devices_all * capacity, BLK, BLK), jnp.float32).at[places]]
    ppermute x6 -> x0, starting transfers between devices: 20.3 us -> none  [shifted(): return lax.ppermute(value, axis, pairs)]
    unnamed x18 -> x1, local copies, waits for them, and re-layouts: 17.6 us -> 1.34 us
    broadcast_in_dim x5 -> x0, local copies, waits for them, and re-layouts: 10.3 us -> none  [the longest x1 7.86 us: per_device(): jnp.zeros((devices_all * capacity, BLK, BLK), jnp.float32).at[places]]
  transfers between devices with their start and end apart: 8 -> 2, of which waited for: 4 -> 1; matrix products, arithmetic and copies ran while one was open for 13% -> 1% of each run, Pallas kernels for 0% -> 32%
where the time goes in v1:
time: 487 us; the launch traced here: 481 us
  waiting for transfers between devices  243 us (50%)
  Pallas kernels  174 us (36%)
  starting transfers between devices  57.2 us (12%)
    all_to_all x1, waiting for transfers between devices, per_device(): lax.all_to_all(send.reshape(DEVICES, 2, BLK, BLK), ('row', 'col'), split_...  243 us
    pallas_call x1, Pallas kernels, per_device(): pl.pallas_call(product_kernel, out_shape=jax.ShapeDtypeStruct((2 * DEVICE...  153 us
    all_to_all x1, starting transfers between devices, per_device(): lax.all_to_all(send.reshape(DEVICES, 2, BLK, BLK), ('row', 'col'), split_...  46.5 us
    pallas_call x1, Pallas kernels, per_device(): pl.pallas_call(add_kernel, out_shape=jax.ShapeDtypeStruct((NBLK, BLK, BLK...  20.4 us
    all_to_all x1, starting transfers between devices, per_device(): lax.all_to_all(send_targets, ('row', 'col'), split_axis=0, concat_axis=0,...  10.8 us
  transfers between devices with their start and end apart: 2, of which 1 were waited for; matrix products, arithmetic and copies ran while one was open for 1% of the time, Pallas kernels for 32%

profile of v1, /device:TPU:18, one launch (start us, length us, event | category | flops | bytes accessed | tf_op | source)
XLA Modules:
  0.0 481.4 jit_solution(17727949094749476676)
XLA Ops:
  0.0 0.7 bitcast_add_fusion
  0.7 0.8 select_reduce_fusion.1
  1.5 0.7 copy.15
  2.2 10.8 %all-to-all-start = ((s32[128,1,2]{2,1,0:T(1,128)}), s32[128,1,2]{2,1,0:T(1,128)}, u32[]{:S(2)}, u32[]{:S(2)}) async-start(s32[128,1,2]{2,1,0:T(1,128)} %copy.15), calls=%async_computation | async-start | bytes 131072 | tf_op jit(solution)/shard_map/all_to_all | solution.py:215
  13.0 0.1 copy.16
  13.1 0.1 stack.29
  13.3 0.6 fusion.1.inv
  13.9 1.3 copy.17.a_occ
  15.2 153.3 %products.1 = f32[256,128,128]{2,1,0:T(8,128)} custom-call(f32[1024,256]{1,0:T(8,128)} %a_ref.1, f32[512,2048]{1,0:T(8,128)} %b_ref.1, s32[8,2]{1,0:T(8,128)} %copy.17.a_occ, s32[4,16]{1,0:T(4,128)} %b_occ.1, s32[256]{0:T(256)} %fusion.1.inv), custom_call_target="tpu_custom_call" | custom-call | tf_op jit(solution)/shard_map/products/pallas_call | solution.py:220
  168.5 0.0 all-to-all-done
  168.5 46.5 %all-to-all-start.1 = ((f32[128,2,128,128]{3,2,1,0:T(8,128)}), f32[128,2,128,128]{3,2,1,0:T(8,128)}, u32[]{:S(2)}, u32[]{:S(2)}) async-start(f32[128,2,128,128]{3,2,1,0:T(8,128)} %bitcast.22), calls=%async_computation.1 | async-start | bytes 33554432 | tf_op jit(solution)/shard_map/all_to_all | solution.py:247
  215.0 0.5 broadcast.159
  215.5 1.6 reduce.3
  217.2 0.7 reshape.228.targets
  217.9 243.1 %all-to-all-done.1 = f32[128,2,128,128]{3,2,1,0:T(8,128)} async-done(((f32[128,2,128,128]{3,2,1,0:T(8,128)}), f32[128,2,128,128]{3,2,1,0:T(8,128)}, u32[]{:S(2)}, u32[]{:S(2)}) %all-to-all-start.1) | async-done | bytes 16777248 | tf_op jit(solution)/shard_map/all_to_all | solution.py:247
  461.0 20.4 %add_blocks.1 = f32[128,128,128]{2,1,0:T(8,128)} custom-call(s32[256]{0:T(256)} %reshape.228.targets, f32[128,128,128]{2,1,0:T(8,128)} %bitcast.23, f32[256,128,128]{2,1,0:T(8,128)} %bitcast.10.got_ref), custom_call_target="tpu_custom_call" | custom-call | tf_op jit(solution)/shard_map/add_blocks/pallas_call | solution.py:251
  (4 shorter events, 0.0 us)
Async XLA Ops:
  2.2 166.3 %all-to-all-start = ((s32[128,1,2]{2,1,0:T(1,128)}), s32[128,1,2]{2,1,0:T(1,128)}, u32[]{:S(2)}, u32[]{:S(2)}) async-start(s32[128,1,2]{2,1,0:T(1,128)} %copy.15), calls=%async_computation | async-start | bytes 131072 | tf_op jit(solution)/shard_map/all_to_all | solution.py:215
  168.5 292.5 %all-to-all-start.1 = ((f32[128,2,128,128]{3,2,1,0:T(8,128)}), f32[128,2,128,128]{3,2,1,0:T(8,128)}, u32[]{:S(2)}, u32[]{:S(2)}) async-start(f32[128,2,128,128]{3,2,1,0:T(8,128)} %bitcast.22), calls=%async_computation.1 | async-start | bytes 33554432 | tf_op jit(solution)/shard_map/all_to_all | solution.py:247

commit v2 on v1

--- a/solution.py
+++ b/solution.py
@@ -12,27 +12,35 @@
 DEVICES = N_ROW * N_COL
 NBLK = 128
 CHUNKS = 4
+ROWS = (48, 40, 40)
+STARTS = (0, 48, 88)
+HOPS = (1, 3, 2)
 MESH = pl.DeviceIdType.MESH
 VMEM_LIMIT = 64 * 1024 * 1024 - 65536
 
 
 def product_kernel(
-    a_ref, b_ref, a_occ, b_occ, inv, s_out,
-    a_own, b_own, b_cross, b_far, a_got, b_got, a_cat, b_cat, prod, staged,
+    a_ref, b_ref, a_occ, b_occ, inv, s0_out, s1_out, s2_out,
+    a_own, b_own, b_cross, b_far, a_got, b_got, a_cat, b_cat, prod, staged0, staged1, staged2,
     a_send, a_recv, b_send, b_recv, x_send, x_recv, out_sem,
 ):
     row = lax.axis_index("row")
     col = lax.axis_index("col")
     half = row // 4
     z = row % 4
+    core = col % 2
     far = (row + 4) % N_ROW
     inner = b_ref.shape[0] // 2
     part = inner // CHUNKS
+    partner = col + 1 - 2 * core
+    across = 3 - 2 * core
 
     barrier = pltpu.get_barrier_semaphore()
     peers = [(half * 4 + (z + d) % 4, col) for d in (1, 2, 3)]
     peers.append((far, col))
-    peers += [(row, (col + d) % N_COL) for d in (1, 2, 3, 13, 14, 15)]
+    peers.append((row, partner))
+    peers += [(row, (col + d) % N_COL) for d in (2, 14)]
+    peers.append((row, (col + 13 + 6 * core) % N_COL))
     for peer in peers:
         pl.semaphore_signal(barrier, inc=1, device_id=peer, device_id_type=MESH)
 
@@ -68,11 +76,15 @@
             device_id=(half * 4 + (z + 4 - t) % 4, col), device_id_type=MESH,
         )
 
-    def left_copy(t):
+    def left_copy(source, to, slot, number):
         return pltpu.make_async_remote_copy(
-            a_own, a_got.at[t - 1], a_send.at[t - 1], a_recv.at[t - 1],
-            device_id=(row, (col + N_COL - t) % N_COL), device_id_type=MESH,
+            source, a_got.at[slot], a_send.at[number], a_recv.at[slot],
+            device_id=(row, to), device_id_type=MESH,
         )
+
+    left_next = left_copy(a_own, (col + 14) % N_COL, 1, 0)
+    left_other = left_copy(a_own, (col + N_COL - across) % N_COL, across - 1, 1)
+    left_pass = left_copy(a_got.at[1], partner, 2 * core, 2)
 
     @pl.when(z < 3)
     def _():
@@ -86,16 +98,13 @@
             ring_copy(b_own, t, pl.ds(0, inner)).start()
 
     def mask_left(n, carry):
-        p = n // 2
         for k in range(2):
-            there = a_occ[p, k].astype(jnp.float32)
-            at = pl.ds(p * BLK, BLK)
+            there = a_occ[n, k].astype(jnp.float32)
+            at = pl.ds(n * BLK, BLK)
             a_own[at, k * BLK:(k + 1) * BLK] = a_ref[at, k * BLK:(k + 1) * BLK] * there
         return carry
 
-    lax.fori_loop(0, 16, mask_left, 0)
-    for t in (1, 2, 3):
-        left_copy(t).start()
+    lax.fori_loop(0, 8, mask_left, 0)
 
     def split_left(read):
         def one(m, carry):
@@ -152,56 +161,185 @@
                 @pl.when(z < t)
                 def _(t=t):
                     ring_copy(b_far, t, pl.ds(c * part, part)).start()
-        for c in range(CHUNKS):
-            cross_copy(c).wait_send()
+
+    left_other.start()
+    left_next.start()
+    left_next.wait_recv()
+    left_pass.start()
 
     for t in (1, 2, 3):
-        left_copy(t).wait_recv()
+        if t != 2:
+            left_copy(a_own, partner, t - 1, 0).wait_recv()
         split_left(lambda at: a_got[t - 1, at, :])
         ring_copy(b_own, t, pl.ds(0, inner)).wait_recv()
         split_right(lambda at: b_got[t - 1, :, at])
         multiply(False)
 
-    def place(group, carry):
-        for k in range(16):
-            n = group * 16 + k
-            staged[n] = prod[inv[n]]
-        at = pl.ds(group * 16, 16)
-        pltpu.make_async_copy(staged.at[at], s_out.at[at], out_sem).start()
-        return carry
-
-    lax.fori_loop(0, 16, place, 0)
+    order = lambda u, v, w: (u * 4 + v) * 4 + w
+    for g, (staged, out) in enumerate(((staged0, s0_out), (staged1, s1_out), (staged2, s2_out))):
+        rows = pl.ds(STARTS[g], ROWS[g])
+
+        def place(group, carry):
+            u, v = group // 4, group % 4
+            for w in range(4):
+                chip = (order(u, v, w), order(w, u, v), order(v, w, u))[g]
+                for k in range(4):
+                    staged[u, v, w, k // 2, k % 2] = prod[inv[chip * 4 + k], rows]
+            pltpu.make_async_copy(staged.at[u, v], out.at[u, v], out_sem.at[g]).start()
+            return carry
+
+        lax.fori_loop(0, 16, place, 0)
+
+    @pl.when(z < 3)
+    def _():
+        for c in range(CHUNKS):
+            cross_copy(c).wait_send()
+
+    left_next.wait_send()
+    left_other.wait_send()
+    left_pass.wait_send()
     for t in (1, 2, 3):
-        left_copy(t).wait_send()
         ring_copy(b_own, t, pl.ds(0, inner)).wait_send()
-    pltpu.make_async_copy(staged, s_out, out_sem).wait()
-
-
-def add_kernel(targets, c_ref, got_ref, out_ref):
+    for g, (staged, out) in enumerate(((staged0, s0_out), (staged1, s1_out), (staged2, s2_out))):
+        pltpu.make_async_copy(staged, out, out_sem.at[g]).wait()
+
+
+def exchange_kernel(*refs):
+    s, r3, r1, r2 = refs[0:4], refs[4:8], refs[8:12], refs[12:16]
+    (s1_send, s1_recv, s2_send, s2_recv, s3_send, s3_recv, c_send, c_recv, own_sem) = refs[16:]
+    routes = range(4)
+    row = lax.axis_index("row")
+    col = lax.axis_index("col")
+    core = col % 2
+    at = (col // 4, (row // 4) * 2 + (col // 2) % 2, row % 4)
+
+    def device(place, c):
+        x, y, z = place
+        return ((y // 2) * 4 + z, x * 4 + (y % 2) * 2 + c)
+
+    def moved(dim, value):
+        return tuple(value if i == dim else at[i] for i in range(3))
+
+    barrier = pltpu.get_barrier_semaphore()
+    peers = [device(at, 1 - core)]
+    for dim in range(3):
+        for hop in HOPS:
+            for c in (core, 1 - core):
+                peers.append(device(moved(dim, (at[dim] + hop) % 4), c))
+    for peer in peers:
+        pl.semaphore_signal(barrier, inc=1, device_id=peer, device_id_type=MESH)
+    pl.semaphore_wait(barrier, len(peers))
+
+    def dims(g):
+        return g % 3, (g + 1) % 3, (g + 2) % 3
+
+    def copy1(g, k):
+        d1 = dims(g)[0]
+        a = (at[d1] + HOPS[k]) % 4
+        return pltpu.make_async_remote_copy(
+            s[g].at[a], r1[g].at[at[d1]], s1_send.at[g], s1_recv.at[g, k],
+            device_id=device(moved(d1, a), core), device_id_type=MESH,
+        )
+
+    def source1(g, k):
+        return (at[dims(g)[0]] + 4 - HOPS[k]) % 4
+
+    def copy2(g, j, k, src, a):
+        d2 = dims(g)[1]
+        b = (at[d2] + HOPS[j]) % 4
+        return pltpu.make_async_remote_copy(
+            src.at[a, b], r2[g].at[at[d2], a], s2_send.at[g], s2_recv.at[g, j, k],
+            device_id=device(moved(d2, b), core), device_id_type=MESH,
+        )
+
+    def send3(g, src, b, a):
+        d3 = dims(g)[2]
+        into = r3[g].at[at[d3], core, b, a]
+        for hop in HOPS:
+            e = (at[d3] + hop) % 4
+            for f in (core, 1 - core):
+                pltpu.make_async_remote_copy(
+                    src.at[e, f], into, s3_send.at[g], s3_recv.at[g],
+                    device_id=device(moved(d3, e), f), device_id_type=MESH,
+                ).start()
+        pltpu.make_async_remote_copy(
+            src.at[at[d3], 1 - core], into, c_send.at[g], c_recv.at[g],
+            device_id=device(at, 1 - core), device_id_type=MESH,
+        ).start()
+        pltpu.make_async_copy(src.at[at[d3], core], into, own_sem.at[g]).start()
+
+    def forward(g, k):
+        a = at[dims(g)[0]] if k == 3 else source1(g, k)
+        src = s[g] if k == 3 else r1[g]
+        for j in range(3):
+            copy2(g, j, k, src, a).start()
+        b = at[dims(g)[1]]
+        send3(g, src.at[a, b], b, a)
+
+    def arrive2(g, k):
+        a = at[dims(g)[0]] if k == 3 else source1(g, k)
+        for j in range(3):
+            b = (at[dims(g)[1]] + 4 - HOPS[j]) % 4
+            copy2(g, j, k, s[g], a).wait_recv()
+            send3(g, r2[g].at[b, a], b, a)
+
+    for k in range(3):
+        for g in routes:
+            copy1(g, k).start()
+    for g in routes:
+        forward(g, 3)
+    before = 3
+    for k in range(3):
+        for g in routes:
+            copy1(g, k).wait_recv()
+            forward(g, k)
+        for g in routes:
+            arrive2(g, before)
+        before = k
+    for g in routes:
+        arrive2(g, before)
+    for g in routes:
+        most = r3[g].at[pl.ds(0, 3)]
+        one = r3[g].at[0, 0]
+        for sem in (s3_recv, s1_send, s2_send, s3_send):
+            pltpu.make_async_copy(most, most, sem.at[g]).wait()
+        for sem in (c_recv, c_send, own_sem):
+            pltpu.make_async_copy(one, one, sem.at[g]).wait()
+
+
+def add_kernel(targets, c_ref, got0, got1, got2, out_ref):
     step = pl.program_id(0)
-    count = got_ref.shape[0]
+    d3, c = step // 2, step % 2
 
     @pl.when(step == 0)
     def _():
         out_ref[...] = c_ref[...]
 
-    def one(k, carry):
-        target = targets[step * count + k]
-
-        @pl.when(target >= 0)
-        def _():
-            out_ref[target] = out_ref[target] + got_ref[k]
-
-        return carry
-
-    lax.fori_loop(0, count, one, 0)
+    for g, got in enumerate((got0, got1, got2)):
+        rows = pl.ds(STARTS[g], ROWS[g])
+
+        def one(n, carry):
+            d2, d1, k = n // 8, (n // 2) % 4, n % 2
+            x, y, z = ((d1, d2, d3), (d3, d1, d2), (d2, d3, d1))[g]
+            target = targets[((z * 2 + c) * 4 + y) * 4 + x, k]
+
+            @pl.when(target >= 0)
+            def _():
+                out_ref[target, rows] = out_ref[target, rows] + got[0, 0, d2, d1, k]
+
+            return carry
+
+        lax.fori_loop(0, 32, one, 0)
 
 
 def per_device(a_panels, b_panels, a_occupancy, b_occupancy, owner_device, owner_block, c_previous):
     owners = owner_device.reshape(NBLK)
     targets = owner_block.reshape(NBLK)
+    o_row, o_col = owners // N_COL, owners % N_COL
+    o_y = (o_row // 4) * 2 + (o_col // 2) % 2
+    places = ((o_col // 4 * 4 + o_y) * 4 + o_row % 4) * 2 + o_col % 2
     number = jnp.arange(NBLK, dtype=jnp.int32)
-    named = owners[:, None] == jnp.arange(DEVICES, dtype=jnp.int32)[None, :]
+    named = places[:, None] == jnp.arange(DEVICES, dtype=jnp.int32)[None, :]
     packed = number * DEVICES + targets
     first = jnp.min(jnp.where(named, packed[:, None], NBLK * DEVICES), axis=0)
     last = jnp.max(jnp.where(named, packed[:, None], -1), axis=0)
@@ -211,15 +349,17 @@
     there = jnp.stack([has_first, has_second], axis=1)
     block = pair // DEVICES
     inv = ((block % 16) * 8 + block // 16).reshape(2 * DEVICES)
-    send_targets = jnp.where(there, pair % DEVICES, -1)
-    got_targets = lax.all_to_all(
-        send_targets, ("row", "col"), split_axis=0, concat_axis=0, tiled=True
-    )
+    send_targets = jnp.pad(
+        jnp.where(there, pair % DEVICES, -1), ((0, 0), (0, BLK - 2)), constant_values=-1
+    ).reshape(4, 4, 4, 2, 1, BLK)
 
     vmem = lambda shape, dtype=jnp.float32: pltpu.VMEM(shape, dtype)
-    send = pl.pallas_call(
+    dma = lambda *shape: pltpu.SemaphoreType.DMA(shape)
+    anywhere = pl.BlockSpec(memory_space=pl.ANY)
+    blocks = lambda lead: [jax.ShapeDtypeStruct(lead + (2, r, BLK), jnp.float32) for r in ROWS]
+    sent = pl.pallas_call(
         product_kernel,
-        out_shape=jax.ShapeDtypeStruct((2 * DEVICES, BLK, BLK), jnp.float32),
+        out_shape=blocks((4, 4, 4, 2)),
         in_specs=[
             pl.BlockSpec(memory_space=pltpu.VMEM),
             pl.BlockSpec(memory_space=pltpu.VMEM),
@@ -227,16 +367,14 @@
             pl.BlockSpec(memory_space=pltpu.SMEM),
             pl.BlockSpec(memory_space=pltpu.SMEM),
         ],
-        out_specs=pl.BlockSpec(memory_space=pl.ANY),
+        out_specs=[anywhere] * 3,
         scratch_shapes=[
             vmem((1024, 256)), vmem((256, 2048)), vmem((256, 2048)), vmem((256, 2048)),
             vmem((3, 1024, 256)), vmem((3, 256, 2048)),
             vmem((1024, 768), jnp.bfloat16), vmem((768, 2048), jnp.bfloat16),
-            vmem((NBLK, BLK, BLK)), vmem((2 * DEVICES, BLK, BLK)),
-            pltpu.SemaphoreType.DMA((3,)), pltpu.SemaphoreType.DMA((3,)),
-            pltpu.SemaphoreType.DMA((3,)), pltpu.SemaphoreType.DMA((3,)),
-            pltpu.SemaphoreType.DMA((CHUNKS,)), pltpu.SemaphoreType.DMA((CHUNKS,)),
-            pltpu.SemaphoreType.DMA,
+            vmem((NBLK, BLK, BLK)),
+            *[vmem((4, 4, 4, 2, 2, r, BLK)) for r in ROWS],
+            dma(3), dma(3), dma(3), dma(3), dma(CHUNKS), dma(CHUNKS), dma(3),
         ],
         compiler_params=pltpu.CompilerParams(
             collective_id=0, has_side_effects=True, vmem_limit_bytes=VMEM_LIMIT
@@ -244,25 +382,38 @@
         name="products",
     )(a_panels, b_panels, a_occupancy, b_occupancy, inv)
 
-    got = lax.all_to_all(
-        send.reshape(DEVICES, 2, BLK, BLK), ("row", "col"), split_axis=0, concat_axis=0, tiled=True
-    ).reshape(2 * DEVICES, BLK, BLK)
+    index = lambda lead: [jax.ShapeDtypeStruct(lead + (1, BLK), jnp.int32)]
+    got = pl.pallas_call(
+        exchange_kernel,
+        out_shape=(
+            blocks((4, 2, 4, 4)) + index((4, 2, 4, 4))
+            + blocks((4, 4, 4, 2)) + index((4, 4, 4, 2))
+            + blocks((4, 4, 4, 2)) + index((4, 4, 4, 2))
+        ),
+        in_specs=[anywhere] * 4,
+        out_specs=[anywhere] * 12,
+        scratch_shapes=[
+            dma(4), dma(4, 3), dma(4), dma(4, 3, 4), dma(4), dma(4), dma(4), dma(4), dma(4),
+        ],
+        compiler_params=pltpu.CompilerParams(collective_id=1, has_side_effects=True),
+        name="exchange",
+    )(*sent, send_targets)
 
     owned = pl.pallas_call(
         add_kernel,
         out_shape=jax.ShapeDtypeStruct((NBLK, BLK, BLK), jnp.float32),
         grid_spec=pltpu.PrefetchScalarGridSpec(
             num_scalar_prefetch=1,
-            grid=(16,),
-            in_specs=[
-                pl.BlockSpec((NBLK, BLK, BLK), lambda i, t: (0, 0, 0)),
-                pl.BlockSpec((16, BLK, BLK), lambda i, t: (i, 0, 0)),
+            grid=(8,),
+            in_specs=[pl.BlockSpec((NBLK, BLK, BLK), lambda i, t: (0, 0, 0))] + [
+                pl.BlockSpec((1, 1, 4, 4, 2, r, BLK), lambda i, t: (i // 2, i % 2, 0, 0, 0, 0, 0))
+                for r in ROWS
             ],
             out_specs=pl.BlockSpec((NBLK, BLK, BLK), lambda i, t: (0, 0, 0)),
         ),
         compiler_params=pltpu.CompilerParams(vmem_limit_bytes=VMEM_LIMIT),
         name="add_blocks",
-    )(got_targets.reshape(2 * DEVICES), c_previous.reshape(NBLK, BLK, BLK), got)
+    )(got[3].reshape(DEVICES, BLK), c_previous.reshape(NBLK, BLK, BLK), *got[:3])
     return owned.reshape(c_previous.shape)
 
 

time: 487 us -> 376 us (0.77)
  waiting for transfers between devices: 243 us -> 0 us
  Pallas kernels: 174 us -> 369 us
  starting transfers between devices: 57.2 us -> 0 us
    all_to_all x2 -> x0, waiting for transfers between devices: 243 us -> none  [the longest x1 243 us: per_device(): lax.all_to_all(send.reshape(DEVICES, 2, BLK, BLK), ('row', 'col'), split_...]
    pallas_call x1 -> x2, Pallas kernels: 153 us -> 334 us  [the longest x1 218 us: per_device(): pl.pallas_call(exchange_kernel, out_shape=blocks((4, 2, 4, 4)) + index((4...]
    all_to_all x2 -> x0, starting transfers between devices: 57.2 us -> none  [the longest x1 46.5 us: per_device(): lax.all_to_all(send.reshape(DEVICES, 2, BLK, BLK), ('row', 'col'), split_...]
    pallas_call x1, Pallas kernels: 20.4 us -> 35.4 us  [per_device(): pl.pallas_call(add_kernel, out_shape=jax.ShapeDtypeStruct((NBLK, BLK, BLK...]
  transfers between devices with their start and end apart: 2 -> 0, of which waited for: 1 -> 0; matrix products, arithmetic and copies ran while one was open for 1% -> 0% of each run, Pallas kernels for 32% -> 0%
where the time goes in v2:
time: 376 us; the launch traced here: 373 us
  Pallas kernels  369 us (98%)
    pallas_call x1, Pallas kernels, per_device(): pl.pallas_call(exchange_kernel, out_shape=blocks((4, 2, 4, 4)) + index((4...  218 us
    pallas_call x1, Pallas kernels, per_device(): pl.pallas_call(product_kernel, out_shape=blocks((4, 4, 4, 2)), in_specs=[...  116 us
    pallas_call x1, Pallas kernels, per_device(): pl.pallas_call(add_kernel, out_shape=jax.ShapeDtypeStruct((NBLK, BLK, BLK...  35.4 us

profile of v2, /device:TPU:18, one launch (start us, length us, event | category | flops | bytes accessed | tf_op | source)
XLA Modules:
  0.0 373.1 jit_solution(1239199708711999202)
XLA Ops:
  0.0 0.7 fusion.5
  0.7 0.1 select_reduce_fusion
  0.9 1.3 copy.14.a_occ
  2.2 0.1 copy.16
  2.3 0.6 pad.4.clone
  3.0 0.1 copy.13
  3.1 0.1 stack.13
  3.2 0.6 fusion.1.inv
  3.8 115.5 %products.1 = (f32[4,4,4,2,2,48,128]{6,5,4,3,2,1,0:T(8,128)}, f32[4,4,4,2,2,40,128]{6,5,4,3,2,1,0:T(8,128)}, f32[4,4,4,2,2,40,128]{6,5,4,3,2,1,0:T(8,128)}) custom-call(f32[1024,256]{1,0:T(8,128)} %a_ref.1, f32[512,2048]{1,0:T(8,128)} %b_ref.1, s32[8,2]{1,0:T(8,128)} %copy.14.a_occ, s32[4,16]{1,0:T(4,128)} %b_occ.1, s32[256]{0:T(256)} %fusion.1.inv), custom_call_target="tpu_custom_call" | custom-call | tf_op jit(solution)/shard_map/products/pallas_call | solution.py:360
  119.3 218.3 %exchange.1 = (f32[4,2,4,4,2,48,128]{6,5,4,3,2,1,0:T(8,128)}, f32[4,2,4,4,2,40,128]{6,5,4,3,2,1,0:T(8,128)}, f32[4,2,4,4,2,40,128]{6,5,4,3,2,1,0:T(8,128)}, s32[...) custom-call(f32[4,4,4,2,2,48,128]{6,5,4,3,2,1,0:T(8,128)} %get-tuple, ...), custom_call_target="tpu_custom_call" | custom-call | tf_op jit(solution)/shard_map/exchange/pallas_call | solution.py:386
  337.6 35.4 %add_blocks.1 = f32[128,128,128]{2,1,0:T(8,128)} custom-call(s32[128,128]{1,0:T(8,128)} %bitcast.34, f32[128,128,128]{2,1,0:T(8,128)} %bitcast.32, f32[4,2,4,4,2,48,128]{6,5,4,3,2,1,0:T(8,128)} %get-tuple-element.16.got0, f32[4,2,4,4,2,40,128]{6,5,4,3,2,1,0:T(8,128)} %get-tuple-element.17.got1, f32[4,2,4,4,2,40,128]{6,5,4,3,2,1,0:T(8,128)} %get-tuple-element.18.got2), custom_call_target="tpu_custom_call" | custom-call | tf_op jit(solution)/shard_map/add_blocks/pallas_call | solution.py:402
  (3 shorter events, 0.0 us)
